TPU v7x, 512 devices: a whole 4x4x16 slice. The times are simulated.
512 devices in a mesh: tx: 8 (over y, core), ty: 8 (over x, z_hi), ang: 8 (over z_lo).
Axes of the slice: x: 4, y: 4, z: 16 (z_hi: 2, z_lo: 8; z = z_hi * 8 + z_lo), core: 2. Of those that a mesh axis runs over, the one named last changes fastest.
Arguments:
- projections: bfloat16 [8, 8, 128, 8, 1024], P('tx', 'ty', 'ang'), may hold values from -6 to 6
- view_angles: float32 [8, 8, 128], P('tx', 'ty', 'ang'), may hold values from -3.140625 to 3.140625
- tilt: float32 [8, 8], P('tx', 'ty'), may hold values from 0.3 to 0.7
- offsets: int32 [8, 8], P('tx', 'ty'), may hold values from 0 to 128
- extents: int32 [8, 8], P('tx', 'ty'), may hold values from 1 to 4
- feather: int32 [8, 8, 2, 4], P('tx', 'ty'), may hold values from 0 to 8
Outputs:
- seams: float32 [8, 8, 8, 4, 1024], P('tx', 'ty', 'ang')
- lower_bands: float32 [8, 8, 8, 4, 1024], P('tx', 'ty', 'ang')
All inputs are finite; a program needn't handle non-finite values.
Results may differ from a plain program's by a relative error of at most 0.0028.
Values sent between devices are 32-bit elements; how exact they have to be, the bound alone decides.
A program may use at most 64 MiB of HBM per device.

v0:
```python
import math

import jax
import jax.numpy as jnp
from jax import lax
from jax.sharding import PartitionSpec as P

PZ = 1
DXMAX = 128


PITCH = 16.0


def passed_along(x, axis, by):
    count = lax.axis_size(axis)
    pairs = [(i, i + by) for i in range(count) if 0 <= i + by < count]
    return lax.ppermute(x, axis, pairs)


def forward_table(width, start, count):
    column = jnp.arange(width, dtype=jnp.int32)[:, None]
    freq = start + jnp.arange(count, dtype=jnp.int32)[None, :]
    turn = (column * freq % width).astype(jnp.float32) * (2.0 * math.pi / width)
    filt = (freq.astype(jnp.float32) + 0.5) / (width // 2) / math.sqrt(width)
    return jnp.concatenate([jnp.cos(turn) * filt, -jnp.sin(turn) * filt], axis=1).astype(
        jnp.bfloat16
    )


def phase_pair(shift, width, start, count):
    freq = (start + jnp.arange(count, dtype=jnp.int32)).astype(jnp.float32)
    turn = shift[..., None] * freq * (2.0 * math.pi / width)
    return (jnp.cos(turn), jnp.sin(turn))


def fourier_sum(proj, angles, lean, planes, width):
    views, rows, _ = proj.shape
    half = width // 2
    block = min(128, half)
    band = rows // 2
    flat = proj.reshape(views * rows, width)
    ycoord = (
        jnp.concatenate(
            [jnp.arange(band, dtype=jnp.int32), width - band + jnp.arange(band, dtype=jnp.int32)]
        ).astype(jnp.float32)
        - width / 2
    )
    zcoord = (jnp.arange(planes, dtype=jnp.int32).astype(jnp.float32) - (planes - 1) / 2) * PITCH
    zshift = lean * jnp.cos(angles)[:, None] * zcoord[None, :]
    yshift = lean * jnp.sin(angles)[:, None] * ycoord[None, :]

    def fourier_one_block(index):
        start = index * block
        table = forward_table(width, start, block)
        spec = jnp.dot(flat, table, preferred_element_type=jnp.float32).reshape(
            views, rows, 2 * block
        )
        spec_re = spec[..., :block]
        spec_im = spec[..., block:]
        ycos, ysin = phase_pair(yshift, width, start, block)
        prod_re = spec_re * ycos - spec_im * ysin
        prod_im = spec_re * ysin + spec_im * ycos
        zcos, zsin = phase_pair(zshift, width, start, block)
        high = lax.Precision.HIGHEST
        real = jnp.einsum("kzf,kyf->zyf", zcos, prod_re, precision=high) - jnp.einsum(
            "kzf,kyf->zyf", zsin, prod_im, precision=high
        )
        imag = jnp.einsum("kzf,kyf->zyf", zcos, prod_im, precision=high) + jnp.einsum(
            "kzf,kyf->zyf", zsin, prod_re, precision=high
        )
        return (real, imag)

    real, imag = lax.map(fourier_one_block, jnp.arange(half // block, dtype=jnp.int32))
    real = jnp.moveaxis(real, 0, 2).reshape(planes, rows, half)
    imag = jnp.moveaxis(imag, 0, 2).reshape(planes, rows, half)
    return (real, imag)


def to_image(real, imag, width):
    half = width // 2
    cols = min(512, width)
    lead = real.shape[:-1]
    left = jnp.concatenate([real, imag], axis=-1).reshape(-1, width)

    def to_one_block(index):
        freq = jnp.arange(half, dtype=jnp.int32)[:, None]
        place = index * cols + jnp.arange(cols, dtype=jnp.int32)[None, :]
        turn = (freq * place % width).astype(jnp.float32) * (2.0 * math.pi / width)
        table = jnp.concatenate([jnp.cos(turn), -jnp.sin(turn)], axis=0) * math.sqrt(2.0 / width)
        return jnp.dot(
            left, table, precision=lax.Precision.HIGHEST, preferred_element_type=jnp.float32
        )

    out = lax.map(to_one_block, jnp.arange(width // cols, dtype=jnp.int32))
    return jnp.moveaxis(out, 0, 1).reshape(lead + (width,))


def on_device(projections, view_angles, tilt, offsets, extents, feather):
    views = projections.shape[2]
    rows = projections.shape[3]
    width = projections.shape[4]
    band = rows // 2
    spread = lax.axis_size("ang")
    planes = PZ * spread
    real, imag = fourier_sum(projections[0, 0], view_angles[0, 0], tilt[0, 0], planes, width)
    real, imag = lax.psum((real, imag), "ang")
    first = lax.axis_index("ang") * PZ
    real = lax.dynamic_slice_in_dim(real, first, PZ, 0)
    imag = lax.dynamic_slice_in_dim(imag, first, PZ, 0)
    scale = 1.0 / math.sqrt(views * spread)
    image = to_image(real * scale, imag * scale, width)
    top = image[:, :band]
    bottom = image[:, band:]
    below = passed_along(bottom, "ty", 1)
    corner = passed_along(below[:, :, :DXMAX], "tx", -1)
    joined = jnp.concatenate([below, corner], axis=2)
    aligned = lax.dynamic_slice_in_dim(joined, offsets[0, 0], width, 2)
    row = jnp.arange(band, dtype=jnp.int32)
    upper = (lax.axis_index("ty") > 0).astype(jnp.float32)
    own = feather[0, 0, 0].astype(jnp.float32)
    other = feather[0, 0, 1].astype(jnp.float32) * (row < extents[0, 0]).astype(jnp.float32) * upper
    total = jnp.maximum(own + other, 1.0)
    seams = (own[None, :, None] * top + other[None, :, None] * aligned) / total[None, :, None]
    return (seams[None, None], bottom[None, None])


def solution(mesh):
    in_specs = (
        P("tx", "ty", "ang", None, None),
        P("tx", "ty", "ang"),
        P("tx", "ty"),
        P("tx", "ty"),
        P("tx", "ty"),
        P("tx", "ty", None, None),
    )
    out_specs = (P("tx", "ty", "ang", None, None), P("tx", "ty", "ang", None, None))
    return jax.shard_map(
        on_device, mesh=mesh, in_specs=in_specs, out_specs=out_specs, check_vma=False
    )
```

profile of v0, /device:TPU:6, one launch (start us, length us, event | category | flops | bytes accessed | tf_op | source)
XLA Modules:
  0.0 283.4 jit_solution(15474160446545390166)
XLA Ops:
  8.7 102.4 %while.28 = (s32[]{:T(128)}, f32[4,8,8,128]{1,2,3,0:T(8,128)S(1)}, f32[4,8,8,128]{1,2,3,0:T(8,128)}, s32[4]{0:T(128)S(1)}, bf16[128,1024]{1,0:T(8,128)(2,1)}, /*...) while((s32[]{:T(128)}, f32[4,8,8,128]{1,2,3,0:T(8,128)S(1)}, ...), condition=%wide.region_1.2_spmd.clone, body=%wide.region_0.1_spmd.clone.sunk | while | flops 77415424 | bytes 6514001 | solution.py:74
  10.0 2.2 multiply_convert_fusion.3
  14.0 4.7 %fusion.97 = f32[128,8,8]{2,1,0:T(8,128)S(1)} fusion(f32[16,8]{0,1:T(8,128)S(1)} %get-tuple-element.314, f32[128]{0:T(128)S(1)} %get-tuple-element.315, f32[16,8,128]{0,1,2:T(8,128)S(1)} %copy.16, f32[16,8,128]{0,1,2:T(8,128)S(1)} %copy.17, f32[16,8]{0,1:T(8,128)S(1)} %get-tuple-element.321), kind=kOutput, calls=%fused_computation.43.clone.1 | convolution fusion | flops 1687552 | bytes 165376 | tf_op jit(solution)/shard_map/while/body/eval_jaxpr/kzf,kyf->zyf/dot_general | solution.py:69
  18.7 6.1 %fusion.98 = f32[4,8,8,128]{1,2,3,0:T(8,128)} fusion(f32[4,8,8,128]{1,2,3,0:T(8,128)} %get-tuple-element.335, s32[]{:T(128)} %get-tuple-element.333, f32[128,8,8]{2,1,0:T(8,128)S(1)} %fusion.97, f32[16,8]{0,1:T(8,128)S(1)} %get-tuple-element.314, f32[128]{0:T(128)S(1)} %get-tuple-element.315, f32[16,8,128]{0,1,2:T(8,128)S(1)} %copy.16, ...), kind=kOutput, calls=%fused_computation.25.clone.1 | convolution fusion | flops 1695744 | bytes 2106880 | tf_op jit(solution)/shard_map/while/body/eval_jaxpr/kzf,kyf->zyf/dot_general | solution.py:69
  24.8 4.7 %fusion.95 = f32[128,8,8]{2,1,0:T(8,128)S(1)} fusion(f32[16,8]{0,1:T(8,128)S(1)} %get-tuple-element.314, f32[128]{0:T(128)S(1)} %get-tuple-element.315, f32[16,8,128]{0,1,2:T(8,128)S(1)} %copy.16, f32[16,8,128]{0,1,2:T(8,128)S(1)} %copy.17, f32[16,8]{0,1:T(8,128)S(1)} %get-tuple-element.321), kind=kOutput, calls=%fused_computation.44.clone.1 | convolution fusion | flops 1687552 | bytes 165376 | tf_op jit(solution)/shard_map/while/body/eval_jaxpr/kzf,kyf->zyf/dot_general | solution.py:66
  29.5 4.7 %fusion.96 = f32[4,8,8,128]{1,2,3,0:T(8,128)S(1)} fusion(f32[4,8,8,128]{1,2,3,0:T(8,128)S(1)} %get-tuple-element.334, s32[]{:T(128)} %get-tuple-element.333, f32[128,8,8]{2,1,0:T(8,128)S(1)} %fusion.95, f32[16,8]{0,1:T(8,128)S(1)} %get-tuple-element.314, f32[128]{0:T(128)S(1)} %get-tuple-element.315, f32[16,8,128]{0,1,2:T(8,128)S(1)} %copy.16, ...), kind=kOutput, calls=%fused_computation.28.clone.1 | convolution fusion | flops 1695744 | bytes 2106372 | tf_op jit(solution)/shard_map/while/body/eval_jaxpr/kzf,kyf->zyf/dot_general | solution.py:66
  35.5 2.2 multiply_convert_fusion.3
  39.6 4.7 %fusion.97 = f32[128,8,8]{2,1,0:T(8,128)S(1)} fusion(f32[16,8]{0,1:T(8,128)S(1)} %get-tuple-element.314, f32[128]{0:T(128)S(1)} %get-tuple-element.315, f32[16,8,128]{0,1,2:T(8,128)S(1)} %copy.16, f32[16,8,128]{0,1,2:T(8,128)S(1)} %copy.17, f32[16,8]{0,1:T(8,128)S(1)} %get-tuple-element.321), kind=kOutput, calls=%fused_computation.43.clone.1 | convolution fusion | flops 1687552 | bytes 165376 | tf_op jit(solution)/shard_map/while/body/eval_jaxpr/kzf,kyf->zyf/dot_general | solution.py:69
  44.3 6.1 %fusion.98 = f32[4,8,8,128]{1,2,3,0:T(8,128)} fusion(f32[4,8,8,128]{1,2,3,0:T(8,128)} %get-tuple-element.335, s32[]{:T(128)} %get-tuple-element.333, f32[128,8,8]{2,1,0:T(8,128)S(1)} %fusion.97, f32[16,8]{0,1:T(8,128)S(1)} %get-tuple-element.314, f32[128]{0:T(128)S(1)} %get-tuple-element.315, f32[16,8,128]{0,1,2:T(8,128)S(1)} %copy.16, ...), kind=kOutput, calls=%fused_computation.25.clone.1 | convolution fusion | flops 1695744 | bytes 2106880 | tf_op jit(solution)/shard_map/while/body/eval_jaxpr/kzf,kyf->zyf/dot_general | solution.py:69
  50.3 4.7 %fusion.95 = f32[128,8,8]{2,1,0:T(8,128)S(1)} fusion(f32[16,8]{0,1:T(8,128)S(1)} %get-tuple-element.314, f32[128]{0:T(128)S(1)} %get-tuple-element.315, f32[16,8,128]{0,1,2:T(8,128)S(1)} %copy.16, f32[16,8,128]{0,1,2:T(8,128)S(1)} %copy.17, f32[16,8]{0,1:T(8,128)S(1)} %get-tuple-element.321), kind=kOutput, calls=%fused_computation.44.clone.1 | convolution fusion | flops 1687552 | bytes 165376 | tf_op jit(solution)/shard_map/while/body/eval_jaxpr/kzf,kyf->zyf/dot_general | solution.py:66
  55.0 4.7 %fusion.96 = f32[4,8,8,128]{1,2,3,0:T(8,128)S(1)} fusion(f32[4,8,8,128]{1,2,3,0:T(8,128)S(1)} %get-tuple-element.334, s32[]{:T(128)} %get-tuple-element.333, f32[128,8,8]{2,1,0:T(8,128)S(1)} %fusion.95, f32[16,8]{0,1:T(8,128)S(1)} %get-tuple-element.314, f32[128]{0:T(128)S(1)} %get-tuple-element.315, f32[16,8,128]{0,1,2:T(8,128)S(1)} %copy.16, ...), kind=kOutput, calls=%fused_computation.28.clone.1 | convolution fusion | flops 1695744 | bytes 2106372 | tf_op jit(solution)/shard_map/while/body/eval_jaxpr/kzf,kyf->zyf/dot_general | solution.py:66
  61.1 2.2 multiply_convert_fusion.3
  65.1 4.7 %fusion.97 = f32[128,8,8]{2,1,0:T(8,128)S(1)} fusion(f32[16,8]{0,1:T(8,128)S(1)} %get-tuple-element.314, f32[128]{0:T(128)S(1)} %get-tuple-element.315, f32[16,8,128]{0,1,2:T(8,128)S(1)} %copy.16, f32[16,8,128]{0,1,2:T(8,128)S(1)} %copy.17, f32[16,8]{0,1:T(8,128)S(1)} %get-tuple-element.321), kind=kOutput, calls=%fused_computation.43.clone.1 | convolution fusion | flops 1687552 | bytes 165376 | tf_op jit(solution)/shard_map/while/body/eval_jaxpr/kzf,kyf->zyf/dot_general | solution.py:69
  69.8 6.1 %fusion.98 = f32[4,8,8,128]{1,2,3,0:T(8,128)} fusion(f32[4,8,8,128]{1,2,3,0:T(8,128)} %get-tuple-element.335, s32[]{:T(128)} %get-tuple-element.333, f32[128,8,8]{2,1,0:T(8,128)S(1)} %fusion.97, f32[16,8]{0,1:T(8,128)S(1)} %get-tuple-element.314, f32[128]{0:T(128)S(1)} %get-tuple-element.315, f32[16,8,128]{0,1,2:T(8,128)S(1)} %copy.16, ...), kind=kOutput, calls=%fused_computation.25.clone.1 | convolution fusion | flops 1695744 | bytes 2106880 | tf_op jit(solution)/shard_map/while/body/eval_jaxpr/kzf,kyf->zyf/dot_general | solution.py:69
  75.9 4.7 %fusion.95 = f32[128,8,8]{2,1,0:T(8,128)S(1)} fusion(f32[16,8]{0,1:T(8,128)S(1)} %get-tuple-element.314, f32[128]{0:T(128)S(1)} %get-tuple-element.315, f32[16,8,128]{0,1,2:T(8,128)S(1)} %copy.16, f32[16,8,128]{0,1,2:T(8,128)S(1)} %copy.17, f32[16,8]{0,1:T(8,128)S(1)} %get-tuple-element.321), kind=kOutput, calls=%fused_computation.44.clone.1 | convolution fusion | flops 1687552 | bytes 165376 | tf_op jit(solution)/shard_map/while/body/eval_jaxpr/kzf,kyf->zyf/dot_general | solution.py:66
  80.6 4.7 %fusion.96 = f32[4,8,8,128]{1,2,3,0:T(8,128)S(1)} fusion(f32[4,8,8,128]{1,2,3,0:T(8,128)S(1)} %get-tuple-element.334, s32[]{:T(128)} %get-tuple-element.333, f32[128,8,8]{2,1,0:T(8,128)S(1)} %fusion.95, f32[16,8]{0,1:T(8,128)S(1)} %get-tuple-element.314, f32[128]{0:T(128)S(1)} %get-tuple-element.315, f32[16,8,128]{0,1,2:T(8,128)S(1)} %copy.16, ...), kind=kOutput, calls=%fused_computation.28.clone.1 | convolution fusion | flops 1695744 | bytes 2106372 | tf_op jit(solution)/shard_map/while/body/eval_jaxpr/kzf,kyf->zyf/dot_general | solution.py:66
  86.6 2.2 multiply_convert_fusion.3
  90.7 4.7 %fusion.97 = f32[128,8,8]{2,1,0:T(8,128)S(1)} fusion(f32[16,8]{0,1:T(8,128)S(1)} %get-tuple-element.314, f32[128]{0:T(128)S(1)} %get-tuple-element.315, f32[16,8,128]{0,1,2:T(8,128)S(1)} %copy.16, f32[16,8,128]{0,1,2:T(8,128)S(1)} %copy.17, f32[16,8]{0,1:T(8,128)S(1)} %get-tuple-element.321), kind=kOutput, calls=%fused_computation.43.clone.1 | convolution fusion | flops 1687552 | bytes 165376 | tf_op jit(solution)/shard_map/while/body/eval_jaxpr/kzf,kyf->zyf/dot_general | solution.py:69
  95.4 6.1 %fusion.98 = f32[4,8,8,128]{1,2,3,0:T(8,128)} fusion(f32[4,8,8,128]{1,2,3,0:T(8,128)} %get-tuple-element.335, s32[]{:T(128)} %get-tuple-element.333, f32[128,8,8]{2,1,0:T(8,128)S(1)} %fusion.97, f32[16,8]{0,1:T(8,128)S(1)} %get-tuple-element.314, f32[128]{0:T(128)S(1)} %get-tuple-element.315, f32[16,8,128]{0,1,2:T(8,128)S(1)} %copy.16, ...), kind=kOutput, calls=%fused_computation.25.clone.1 | convolution fusion | flops 1695744 | bytes 2106880 | tf_op jit(solution)/shard_map/while/body/eval_jaxpr/kzf,kyf->zyf/dot_general | solution.py:69
  101.4 4.7 %fusion.95 = f32[128,8,8]{2,1,0:T(8,128)S(1)} fusion(f32[16,8]{0,1:T(8,128)S(1)} %get-tuple-element.314, f32[128]{0:T(128)S(1)} %get-tuple-element.315, f32[16,8,128]{0,1,2:T(8,128)S(1)} %copy.16, f32[16,8,128]{0,1,2:T(8,128)S(1)} %copy.17, f32[16,8]{0,1:T(8,128)S(1)} %get-tuple-element.321), kind=kOutput, calls=%fused_computation.44.clone.1 | convolution fusion | flops 1687552 | bytes 165376 | tf_op jit(solution)/shard_map/while/body/eval_jaxpr/kzf,kyf->zyf/dot_general | solution.py:66
  106.2 4.7 %fusion.96 = f32[4,8,8,128]{1,2,3,0:T(8,128)S(1)} fusion(f32[4,8,8,128]{1,2,3,0:T(8,128)S(1)} %get-tuple-element.334, s32[]{:T(128)} %get-tuple-element.333, f32[128,8,8]{2,1,0:T(8,128)S(1)} %fusion.95, f32[16,8]{0,1:T(8,128)S(1)} %get-tuple-element.314, f32[128]{0:T(128)S(1)} %get-tuple-element.315, f32[16,8,128]{0,1,2:T(8,128)S(1)} %copy.16, ...), kind=kOutput, calls=%fused_computation.28.clone.1 | convolution fusion | flops 1695744 | bytes 2106372 | tf_op jit(solution)/shard_map/while/body/eval_jaxpr/kzf,kyf->zyf/dot_general | solution.py:66
  111.1 1.4 copy.10
  112.4 2.8 copy.11
  116.0 126.3 %all-reduce.3.cloned.1.call-done = (f32[8,8,512]{2,1,0:T(8,128)}, f32[8,8,512]{2,1,0:T(8,128)}) async-done(((f32[8,8,512]{2,1,0:T(8,128)}, f32[8,8,512]{2,1,0:T(8,128)}), (f32[8,8,512]{2,1,0:T(8,128)}, f32[8,8,512]{2,1,0:T(8,128)})) %all-reduce.3.cloned.1.call-update) | async-done | bytes 262160 | tf_op jit(solution)/shard_map/psum | solution.py:107
  243.7 13.2 %while.27 = (s32[]{:T(128)}, f32[2,8,512]{2,1,0:T(8,128)S(1)}, s32[2]{0:T(128)S(1)}, f32[8,1024]{1,0:T(8,128)S(1)}, s32[]{:T(128)}, /*index=5*/s32[1]{0:T(128)}) while((s32[]{:T(128)}, f32[2,8,512]{2,1,0:T(8,128)S(1)}, s32[2]{0:T(128)S(1)}, f32[8,1024]{1,0:T(8,128)S(1)}, s32[]{:T(128)}, /*index=5*/s32[1]{0:T(128)}) %tuple.76), condition=%wide.region_5.6_spmd, body=%wide.region_4.5_spmd.sunk | while | flops 55312896 | bytes 4247653 | solution.py:95
  245.0 4.1 %fusion.86 = (f32[512,512]{1,0:T(8,128)S(1)}, f32[512,512]{1,0:T(8,128)S(1)}) fusion(s32[512]{0:T(512)S(1)} %iota_add_fusion.5), kind=kLoop, calls=%fused_computation.19.clone.1 | loop fusion | flops 3932160 | bytes 2099200 | tf_op jit(solution)/shard_map/while/body/eval_jaxpr/cos | solution.py:90
  249.1 1.2 fusion.87
  251.6 4.1 %fusion.86 = (f32[512,512]{1,0:T(8,128)S(1)}, f32[512,512]{1,0:T(8,128)S(1)}) fusion(s32[512]{0:T(512)S(1)} %iota_add_fusion.5), kind=kLoop, calls=%fused_computation.19.clone.1 | loop fusion | flops 3932160 | bytes 2099200 | tf_op jit(solution)/shard_map/while/body/eval_jaxpr/cos | solution.py:90
  255.7 1.2 fusion.87
  257.6 5.2 %collective-permute-start = (f32[1,4,1024]{2,1,0:T(4,128)S(1)}, f32[1,4,1024]{2,1,0:T(4,128)S(1)}, u32[]{:S(2)}, u32[]{:S(2)}) collective-permute-start(f32[1,4,1024]{2,1,0:T(4,128)S(1)} %get-tuple-element.217), channel_id=1, source_target_pairs={{0,8},{8,16},{16,24},{24,32},{32,40},{40,48},{48,56},{1,9},{9,17},... | collective-permute-start | bytes 49160 | tf_op jit(solution)/shard_map/ppermute | solution.py:18
  262.9 10.0 %collective-permute-done = f32[1,4,1024]{2,1,0:T(4,128)S(1)} collective-permute-done((f32[1,4,1024]{2,1,0:T(4,128)S(1)}, f32[1,4,1024]{2,1,0:T(4,128)S(1)}, u32[]{:S(2)}, u32[]{:S(2)}) %collective-permute-start) | collective-permute-done | bytes 16416 | tf_op jit(solution)/shard_map/ppermute | solution.py:18
  272.8 1.3 collective-permute-start.1
  (58 shorter events, 15.4 us)
Async XLA Ops:
  7.2 235.1 %all-reduce.3.cloned.1.call-start = ((), (), s32[]{:S(2)}) async-start(), calls=%async_computation | async-start | bytes 524288 | tf_op jit(solution)/shard_map/psum | solution.py:107
  243.7 19.1 %copy-start = (s32[1,1,2,4]{3,2,1,0:T(2,128)S(1)}, s32[1,1,2,4]{3,2,1,0:T(2,128)}, u32[]{:S(2)}) copy-start(s32[1,1,2,4]{3,2,1,0:T(2,128)} %param.15) | copy-start | bytes 100
  257.6 15.2 %collective-permute-start = (f32[1,4,1024]{2,1,0:T(4,128)S(1)}, f32[1,4,1024]{2,1,0:T(4,128)S(1)}, u32[]{:S(2)}, u32[]{:S(2)}) collective-permute-start(f32[1,4,1024]{2,1,0:T(4,128)S(1)} %get-tuple-element.217), channel_id=1, source_target_pairs={{0,8},{8,16},{16,24},{24,32},{32,40},{40,48},{48,56},{1,9},{9,17},... | collective-permute-start | bytes 49160 | tf_op jit(solution)/shard_map/ppermute | solution.py:18
  272.8 3.0 %collective-permute-start.1 = (f32[1,4,128]{2,1,0:T(4,128)S(1)}, f32[1,4,128]{2,1,0:T(4,128)S(1)}, u32[]{:S(2)}, u32[]{:S(2)}) collective-permute-start(f32[1,4,128]{2,1,0:T(4,128)S(1)} %slice.38), channel_id=1, source_target_pairs={{64,0},{128,64},{192,128},{256,192},{320,256},{384,320},{448,384},... | collective-permute-start | bytes 6152 | tf_op jit(solution)/shard_map/ppermute | solution.py:18
Sparse Core Ops, SparseCore 0:
  115.4 126.8 all-reduce.2
where the time goes:
time: 286 us; the launch traced here: 283 us
  waiting for transfers between devices  137 us (48%)
  matrix products  88 us (31%)
  other arithmetic  20.5 us (7%)
  between operations  16.1 us (6%)
  local copies, waits for them, and re-layouts  10.3 us (4%)
  starting transfers between devices  6.55 us (2%)
  loops' own time  4.48 us (2%)
    psum x1, waiting for transfers between devices, on_device(): real, imag = lax.psum((real, imag), 'ang')  126 us
    dot_general x4, matrix products, fourier_one_block(): jnp.einsum('kzf,kyf->zyf', zsin, prod_re, precision=high)  24.2 us
    dot_general x4, matrix products, fourier_one_block(): jnp.einsum('kzf,kyf->zyf', zsin, prod_im, precision=high)  18.9 us
    dot_general x4, matrix products, fourier_one_block(): jnp.einsum('kzf,kyf->zyf', zcos, prod_re, precision=high)  18.8 us
    dot_general x4, matrix products, fourier_one_block(): jnp.einsum('kzf,kyf->zyf', zcos, prod_im, precision=high)  18.8 us
    ppermute x2, waiting for transfers between devices, passed_along(): return lax.ppermute(x, axis, pairs)  11.1 us
    another operation x6, other arithmetic  9 us
    cos x2, other arithmetic, to_one_block(): jnp.cos(turn)  8.25 us
  transfers between devices with their start and end apart: 3, of which 3 were waited for; matrix products, arithmetic and copies ran while one was open for 0% of the time, Pallas kernels for 0%

commit v1 on v0

v1 whole, which is shorter than its diff:
```python
import functools
import math

import jax
import jax.numpy as jnp
import ml_dtypes
import numpy as np
from jax import lax
from jax.experimental import pallas as pl
from jax.experimental.pallas import tpu as pltpu
from jax.sharding import PartitionSpec as P

MESH = pl.DeviceIdType.MESH
PITCH = 16.0
U = 1024
F = U // 2
BLOCK = 128
DXMAX = 128

SIN_HALF = (3.1415926401307073, -5.167710083507923, 2.5500775232148563, -0.5982912856211671, 0.07765766030589402)
COS_HALF = (0.9999999532476085, -4.934792830619664, 4.058411352862771, -1.3318765680813944, 0.21968961109803095)


def frequency_order():
    return np.concatenate([np.arange(0, F, 2), np.arange(1, F, 2)])


def forward_half_table():
    freq = frequency_order()[None, :]
    column = np.arange(U // 2)[:, None]
    turn = (column * freq % U) * (2.0 * math.pi / U)
    filt = (freq + 0.5) / F / math.sqrt(U)
    both = np.concatenate([np.cos(turn) * filt, -np.sin(turn) * filt], axis=1)
    return both.astype(np.float32).astype(ml_dtypes.bfloat16)


def inverse_half_tables(views):
    scale = math.sqrt(2.0 / U) / math.sqrt(views)
    place = np.arange(U // 2)[None, :]
    halves = []
    for start in (0, 1):
        freq = np.arange(start, F, 2)[:, None]
        turn = (freq * place % U) * (2.0 * math.pi / U)
        halves.append(np.concatenate([np.cos(turn), -np.sin(turn)], axis=0) * scale)
    return np.stack(halves).astype(np.float32).astype(ml_dtypes.bfloat16)


def horner(z, coefficients):
    total = jnp.full_like(z, coefficients[-1])
    for c in coefficients[-2::-1]:
        total = total * z + c
    return total


def cos_sin_turns(t):
    r = t - jnp.round(t)
    z = r * r
    s = r * horner(z, SIN_HALF)
    c = horner(z, COS_HALF)
    return 1.0 - 2.0 * (s * s), 2.0 * (s * c)


def cos_sin_angle(theta):
    h = theta * 0.5
    z = h * h
    s = h * horner(z, [(-1.0) ** n / math.factorial(2 * n + 1) for n in range(8)])
    c = horner(z, [(-1.0) ** n / math.factorial(2 * n) for n in range(9)])
    return 1.0 - 2.0 * (s * s), 2.0 * (s * c)


def kernel(
    sizes, views,
    x_hbm, g_hbm, t_hbm, angles_ref, tilt_ref, offset_ref, extent_ref, feather_ref,
    seams_ref, lower_ref,
    x_buf, g_buf, t_buf, spec_buf, ycos, ysin, zcos, zsin, col_buf, q_buf,
    bot, top, bot_in, top_in, bot_sum, below_in, corner_in,
    load_sem, send_sem, recv_sem,
):
    n_tx, n_ty, n_ang = sizes
    tx, ty, me = lax.axis_index("tx"), lax.axis_index("ty"), lax.axis_index("ang")
    ty_prev, ty_next = lax.rem(ty + n_ty - 1, n_ty), lax.rem(ty + 1, n_ty)
    tx_prev, tx_next = lax.rem(tx + n_tx - 1, n_tx), lax.rem(tx + 1, n_tx)

    barrier = pltpu.get_barrier_semaphore()
    for d in range(1, n_ang):
        peer = lax.rem(me + d, n_ang)
        pl.semaphore_signal(barrier, inc=1, device_id=(tx, ty, peer), device_id_type=MESH)
    pl.semaphore_signal(barrier, inc=1, device_id=(tx, ty_prev, me), device_id_type=MESH)
    pl.semaphore_signal(barrier, inc=1, device_id=(tx_next, ty_prev, me), device_id_type=MESH)

    load_x = pltpu.make_async_copy(x_hbm, x_buf, load_sem.at[0])
    load_g = pltpu.make_async_copy(g_hbm, g_buf, load_sem.at[1])
    load_t = pltpu.make_async_copy(t_hbm, t_buf, load_sem.at[2])
    load_x.start()
    load_g.start()
    load_t.start()

    lean = tilt_ref[0, 0]
    rows_i = lax.broadcasted_iota(jnp.int32, (views, views), 0)
    cols_i = lax.broadcasted_iota(jnp.int32, (views, views), 1)
    spread = jnp.where(rows_i == cols_i, jnp.broadcast_to(angles_ref[...], (views, views)), 0.0)
    theta = jnp.broadcast_to(jnp.sum(spread, axis=1, keepdims=True), (views, BLOCK))
    cth, sth = cos_sin_angle(theta)
    col_buf[...] = sth * lean
    zcoef = cth * (lean * (0.5 * PITCH / U))
    band = 4
    sub = lax.broadcasted_iota(jnp.int32, (8, BLOCK), 0)
    ycoord = jnp.where(sub < band, sub, sub + (U - 2 * band)) - U // 2
    ycoef = ycoord.astype(jnp.float32) * (1.0 / U)
    lane = lax.broadcasted_iota(jnp.int32, (8, BLOCK), 1)
    for i in range(4):
        at = slice(BLOCK * i, BLOCK * (i + 1))
        freq8 = (lane * 2 + (2 * BLOCK * (i % 2) + i // 2)).astype(jnp.float32)
        freq = jnp.concatenate([freq8] * (views // 8), axis=0)
        c1, s1 = cos_sin_turns(zcoef * freq)
        c2, s2 = 1.0 - 2.0 * (s1 * s1), 2.0 * (s1 * c1)
        c, s = c1, s1
        for j in range(4):
            zcos[j, :, at] = c
            zsin[j, :, at] = s
            if j < 3:
                c, s = c * c2 - s * s2, c * s2 + s * c2
        for k in range(views):
            slope = jnp.broadcast_to(col_buf[k : k + 1, :], (8, BLOCK)) * ycoef
            c, s = cos_sin_turns(slope * freq8)
            ycos[8 * k : 8 * k + 8, at] = c
            ysin[8 * k : 8 * k + 8, at] = s

    load_x.wait()
    load_g.wait()
    rows = views * 8
    left = x_buf[:, :, : U // 2].reshape(rows, U // 2)
    right = x_buf[:, :, U // 2 :].reshape(rows, U // 2)
    spec_buf[...] = jnp.dot(
        jnp.concatenate([left, right], axis=0), g_buf[...], preferred_element_type=jnp.float32
    )

    for i in range(4):
        at = slice(BLOCK * i, BLOCK * (i + 1))
        at_im = slice(F + BLOCK * i, F + BLOCK * (i + 1))
        acc = [[jnp.zeros((8, BLOCK), jnp.float32) for _ in range(4)] for _ in range(4)]
        for k in range(views):
            here, there = slice(8 * k, 8 * k + 8), slice(rows + 8 * k, rows + 8 * k + 8)
            if i < 2:
                s_re = spec_buf[here, at] + spec_buf[there, at]
                s_im = spec_buf[here, at_im] + spec_buf[there, at_im]
            else:
                s_re = spec_buf[here, at] - spec_buf[there, at]
                s_im = spec_buf[here, at_im] - spec_buf[there, at_im]
            yc, ys = ycos[here, at], ysin[here, at]
            p_re = s_re * yc - s_im * ys
            p_im = s_re * ys + s_im * yc
            for j in range(4):
                c = jnp.broadcast_to(zcos[j, k : k + 1, at], (8, BLOCK))
                s = jnp.broadcast_to(zsin[j, k : k + 1, at], (8, BLOCK))
                acc[j][0] += c * p_re
                acc[j][1] += c * p_im
                acc[j][2] += s * p_re
                acc[j][3] += s * p_im
        part, col = i // 2, BLOCK * (i % 2)
        for j in range(4):
            c_re, c_im, s_re, s_im = acc[j]
            for plane, re, im in (
                (4 + j, c_re - s_im, c_im + s_re),
                (3 - j, c_re + s_im, c_im - s_re),
            ):
                at_row = slice(8 * plane, 8 * plane + 8)
                q_buf[part, at_row, col : col + BLOCK] = re
                q_buf[part, at_row, F // 2 + col : F // 2 + col + BLOCK] = im

    load_t.wait()
    halves = []
    for part in range(2):
        q = q_buf[part]
        high = q.astype(jnp.bfloat16)
        low = (q - high.astype(jnp.float32)).astype(jnp.bfloat16)
        both = jnp.dot(
            jnp.concatenate([high, low], axis=0), t_buf[part], preferred_element_type=jnp.float32
        )
        halves.append(both[: 8 * 8] + both[8 * 8 :])
    first, second = halves[0] + halves[1], halves[0] - halves[1]
    sub_wide = lax.broadcasted_iota(jnp.int32, (8, F), 0)
    upper = sub_wide < band
    for plane in range(8):
        a, b = first[8 * plane : 8 * plane + 8], second[8 * plane : 8 * plane + 8]
        bot[plane] = jnp.where(upper, pltpu.roll(a, band, 0), b)
        top[plane] = jnp.where(upper, a, pltpu.roll(b, band, 0))

    pl.semaphore_wait(barrier, n_ang + 1)

    order = sorted(range(1, n_ang), key=lambda d: abs(d - n_ang // 2))
    copies = []
    for which, (src, dst) in enumerate(((bot, bot_in), (top, top_in))):
        group = []
        for d in order:
            peer = lax.rem(me + d, n_ang)
            copy = pltpu.make_async_remote_copy(
                src_ref=src.at[peer], dst_ref=dst.at[d - 1],
                send_sem=send_sem.at[which * n_ang + d], recv_sem=recv_sem.at[which * n_ang + d],
                device_id=(tx, ty, peer), device_id_type=MESH,
            )
            copy.start()
            group.append(copy)
        copies.append(group)

    def gathered(which, mine, landed):
        total = mine[me]
        for d, copy in zip(order, copies[which]):
            copy.wait_recv()
            total += landed[d - 1]
        return total

    bottom = gathered(0, bot, bot_in)
    bot_sum[...] = bottom
    down = pltpu.make_async_remote_copy(
        src_ref=bot_sum, dst_ref=below_in, send_sem=send_sem.at[0], recv_sem=recv_sem.at[0],
        device_id=(tx, ty_next, me), device_id_type=MESH,
    )
    across = pltpu.make_async_remote_copy(
        src_ref=bot_sum.at[:, pl.ds(0, BLOCK)], dst_ref=corner_in,
        send_sem=send_sem.at[n_ang], recv_sem=recv_sem.at[n_ang],
        device_id=(tx_prev, ty_next, me), device_id_type=MESH,
    )
    across.start()
    down.start()

    lower_ref[:, :F] = bottom[:band]
    lower_ref[:, F:] = pltpu.roll(bottom, band, 0)[:band]
    own_top = gathered(1, top, top_in)

    row = sub % band
    own = jnp.zeros((8, BLOCK), jnp.float32)
    other = jnp.zeros((8, BLOCK), jnp.float32)
    seen = (ty > 0).astype(jnp.int32)
    for r in range(band):
        a = feather_ref[0, 0, r].astype(jnp.float32)
        b = (feather_ref[0, 1, r] * (r < extent_ref[0, 0]).astype(jnp.int32) * seen).astype(jnp.float32)
        own = jnp.where(row == r, a, own)
        other = jnp.where(row == r, b, other)
    total = jnp.maximum(own + other, 1.0)
    own, other = own / total, other / total
    shift = offset_ref[0, 0]
    turn_by = (BLOCK - shift) & (BLOCK - 1)

    across.wait_recv()
    down.wait_recv()
    below = below_in[...]
    corner = jnp.where(tx < n_tx - 1, corner_in[...], 0.0)
    tail = pltpu.roll(jnp.where(sub < band, corner, below[:, :BLOCK]), band, 0)
    pieces = [below[:, BLOCK * i : BLOCK * (i + 1)] for i in range(4)] + [tail]
    turned = [pltpu.roll(piece, turn_by, 1) for piece in pieces]
    for i in range(4):
        aligned = jnp.where(lane < BLOCK - shift, turned[i], turned[i + 1])
        seam = own * own_top[:, BLOCK * i : BLOCK * (i + 1)] + other * aligned
        seams_ref[:, BLOCK * i : BLOCK * (i + 1)] = seam[:band]
        seams_ref[:, F + BLOCK * i : F + BLOCK * (i + 1)] = pltpu.roll(seam, band, 0)[:band]

    for group in copies:
        for copy in group:
            copy.wait_send()
    across.wait_send()
    down.wait_send()


def solution(mesh):
    sizes = tuple(mesh.shape[name] for name in ("tx", "ty", "ang"))
    n_ang = sizes[2]

    def on_device(projections, view_angles, tilt, offsets, extents, feather):
        _, _, views, rows, width = projections.shape
        band = rows // 2
        g = jnp.asarray(forward_half_table())
        t = jnp.asarray(inverse_half_tables(views * n_ang))
        smem = pl.BlockSpec(memory_space=pltpu.SMEM)
        vmem = pl.BlockSpec(memory_space=pltpu.VMEM)
        hbm = pl.BlockSpec(memory_space=pl.ANY)
        f32 = jnp.float32
        seams, lower = pl.pallas_call(
            functools.partial(kernel, sizes, views),
            out_shape=[jax.ShapeDtypeStruct((band, width), f32)] * 2,
            in_specs=[hbm, hbm, hbm, vmem, smem, smem, smem, smem],
            out_specs=[vmem, vmem],
            scratch_shapes=[
                pltpu.VMEM((views, rows, width), jnp.bfloat16),
                pltpu.VMEM((F, width), jnp.bfloat16),
                pltpu.VMEM((2, F, F), jnp.bfloat16),
                pltpu.VMEM((2 * views * rows, width), f32),
                pltpu.VMEM((views * rows, F), f32),
                pltpu.VMEM((views * rows, F), f32),
                pltpu.VMEM((4, views, F), f32),
                pltpu.VMEM((4, views, F), f32),
                pltpu.VMEM((views, BLOCK), f32),
                pltpu.VMEM((2, n_ang * rows, F), f32),
                pltpu.VMEM((n_ang, rows, F), f32),
                pltpu.VMEM((n_ang, rows, F), f32),
                pltpu.VMEM((n_ang - 1, rows, F), f32),
                pltpu.VMEM((n_ang - 1, rows, F), f32),
                pltpu.VMEM((rows, F), f32),
                pltpu.VMEM((rows, F), f32),
                pltpu.VMEM((rows, BLOCK), f32),
                pltpu.SemaphoreType.DMA((3,)),
                pltpu.SemaphoreType.DMA((2 * n_ang,)),
                pltpu.SemaphoreType.DMA((2 * n_ang,)),
            ],
            compiler_params=pltpu.CompilerParams(collective_id=0, has_side_effects=True),
        )(projections[0, 0], g, t, view_angles[0], tilt, offsets, extents, feather[0])
        return (seams[None, None, None], lower[None, None, None])

    in_specs = (
        P("tx", "ty", "ang", None, None),
        P("tx", "ty", "ang"),
        P("tx", "ty"),
        P("tx", "ty"),
        P("tx", "ty"),
        P("tx", "ty", None, None),
    )
    out_specs = (P("tx", "ty", "ang", None, None), P("tx", "ty", "ang", None, None))
    return jax.shard_map(
        on_device, mesh=mesh, in_specs=in_specs, out_specs=out_specs, check_vma=False
    )
```

time: 286 us -> 41.6 us (0.15)
  the two profiles are of different devices: /device:TPU:6 before, /device:TPU:1 now
where the time goes in v1:
time: 41.6 us; the launch traced here: 41.4 us
  Pallas kernels  36.9 us (89%)
  between operations  2.58 us (6%)
  local copies, waits for them, and re-layouts  1.94 us (5%)
    pallas_call x1, Pallas kernels, on_device(): pl.pallas_call(functools.partial(kernel, sizes, views), out_shape=[jax.Sh...  36.9 us
    unnamed x4, local copies, waits for them, and re-layouts  1.94 us

profile of v1, /device:TPU:1, one launch (start us, length us, event | category | flops | bytes accessed | tf_op | source)
XLA Modules:
  0.0 41.4 jit_solution(6029175443438964667)
XLA Ops:
  2.6 36.9 %shard_map.95 = (f32[4,1024]{1,0:T(4,128)}, f32[4,1024]{1,0:T(4,128)}) custom-call(bf16[16,8,1024]{2,1,0:T(8,128)(2,1)} %bitcast.5, bf16[512,1024]{1,0:T(8,128)(2,1)} %constant.4.clone.g_hbm, bf16[2,512,512]{2,1,0:T(8,128)(2,1)} %constant.5.clone.t_hbm, f32[1,16]{1,0:T(1,128)} %bitcast.9, f32[1,1]{1,0:T(1,128)S(6)} %copy.12.tilt_ref, ...), custom_call_target="tpu_custom_call" | custom-call | tf_op jit(solution)/shard_map/pallas_call | solution.py:278
  39.4 0.0 copy-start
  39.4 1.3 %copy.15 = f32[1,1,1,4,1024]{4,3,2,1,0:T(4,128)} copy(f32[1,1,1,4,1024]{4,3,2,1,0:T(4,128)} %bitcast.7) | data formatting | bytes 32768
  40.8 0.0 copy-done
  40.8 0.6 %copy.16 = f32[1,1,1,4,1024]{4,3,2,1,0:T(4,128)} copy(f32[1,1,1,4,1024]{4,3,2,1,0:T(4,128)S(1)} %bitcast.6) | data formatting | bytes 32768
Async XLA Ops:
  39.4 1.3 %copy-start = (f32[4,1024]{1,0:T(4,128)S(1)}, f32[4,1024]{1,0:T(4,128)}, u32[]{:S(2)}) copy-start(f32[4,1024]{1,0:T(4,128)} %get-tuple-element.5) | copy-start | bytes 49156

commit v2 on v1

--- a/solution.py
+++ b/solution.py
@@ -70,24 +70,49 @@
 
 def kernel(
     sizes, views,
-    x_hbm, g_hbm, t_hbm, angles_ref, tilt_ref, offset_ref, extent_ref, feather_ref,
+    x_hbm, g_hbm, t_hbm, angles_hbm, tilt_hbm, offset_hbm, extent_hbm, feather_hbm,
     seams_ref, lower_ref,
-    x_buf, g_buf, t_buf, spec_buf, ycos, ysin, zcos, zsin, col_buf, q_buf,
-    bot, top, bot_in, top_in, bot_sum, below_in, corner_in,
-    load_sem, send_sem, recv_sem,
+    angles_ref, tilt_ref, offset_ref, extent_ref, feather_ref, x_buf, g_buf, t_buf, spec_buf, ycos, ysin, zcos, zsin, col_buf, q_buf,
+    bot, top, bot_in, top_in, bot_sum, top_sum, cross_in, below_buf, corner_in,
+    load_sem, small_sem, send_sem, recv_sem, ready_sem,
 ):
     n_tx, n_ty, n_ang = sizes
     tx, ty, me = lax.axis_index("tx"), lax.axis_index("ty"), lax.axis_index("ang")
-    ty_prev, ty_next = lax.rem(ty + n_ty - 1, n_ty), lax.rem(ty + 1, n_ty)
     tx_prev, tx_next = lax.rem(tx + n_tx - 1, n_tx), lax.rem(tx + 1, n_tx)
+    early, late = lax.rem(ty, 2) == 0, lax.rem(ty, 2) == 1
+    has_above = ty > 0
+    late_sends = late & (ty < n_ty - 1)
 
     barrier = pltpu.get_barrier_semaphore()
+
+    def greet(*device):
+        pl.semaphore_signal(barrier, inc=1, device_id=device, device_id_type=MESH)
+
     for d in range(1, n_ang):
-        peer = lax.rem(me + d, n_ang)
-        pl.semaphore_signal(barrier, inc=1, device_id=(tx, ty, peer), device_id_type=MESH)
-    pl.semaphore_signal(barrier, inc=1, device_id=(tx, ty_prev, me), device_id_type=MESH)
-    pl.semaphore_signal(barrier, inc=1, device_id=(tx_next, ty_prev, me), device_id_type=MESH)
-
+        greet(tx, ty, lax.rem(me + d, n_ang))
+
+    @pl.when(has_above)
+    def _():
+        greet(tx_next, ty, me)
+
+    @pl.when(early)
+    def _():
+        greet(tx, ty + 1, me)
+
+    @pl.when(early & has_above)
+    def _():
+        for a in range(n_ang):
+            greet(tx, ty - 1, a)
+
+    small = [
+        pltpu.make_async_copy(src, dst, small_sem.at[n])
+        for n, (src, dst) in enumerate((
+            (angles_hbm, angles_ref), (tilt_hbm, tilt_ref), (offset_hbm, offset_ref),
+            (extent_hbm, extent_ref), (feather_hbm, feather_ref),
+        ))
+    ]
+    for copy in small:
+        copy.start()
     load_x = pltpu.make_async_copy(x_hbm, x_buf, load_sem.at[0])
     load_g = pltpu.make_async_copy(g_hbm, g_buf, load_sem.at[1])
     load_t = pltpu.make_async_copy(t_hbm, t_buf, load_sem.at[2])
@@ -95,6 +120,8 @@
     load_g.start()
     load_t.start()
 
+    small[0].wait()
+    small[1].wait()
     lean = tilt_ref[0, 0]
     rows_i = lax.broadcasted_iota(jnp.int32, (views, views), 0)
     cols_i = lax.broadcasted_iota(jnp.int32, (views, views), 1)
@@ -186,48 +213,99 @@
         bot[plane] = jnp.where(upper, pltpu.roll(a, band, 0), b)
         top[plane] = jnp.where(upper, a, pltpu.roll(b, band, 0))
 
-    pl.semaphore_wait(barrier, n_ang + 1)
-
-    order = sorted(range(1, n_ang), key=lambda d: abs(d - n_ang // 2))
-    copies = []
-    for which, (src, dst) in enumerate(((bot, bot_in), (top, top_in))):
-        group = []
-        for d in order:
-            peer = lax.rem(me + d, n_ang)
-            copy = pltpu.make_async_remote_copy(
-                src_ref=src.at[peer], dst_ref=dst.at[d - 1],
-                send_sem=send_sem.at[which * n_ang + d], recv_sem=recv_sem.at[which * n_ang + d],
-                device_id=(tx, ty, peer), device_id_type=MESH,
-            )
-            copy.start()
-            group.append(copy)
-        copies.append(group)
-
-    def gathered(which, mine, landed):
-        total = mine[me]
-        for d, copy in zip(order, copies[which]):
-            copy.wait_recv()
-            total += landed[d - 1]
+    greeted = n_ang - 1 + has_above.astype(jnp.int32) + late.astype(jnp.int32)
+    pl.semaphore_wait(barrier, greeted + n_ang * late_sends.astype(jnp.int32))
+
+    bands = ((0, bot, bot_in), (1, top, top_in))
+
+    def piece(which, src, dst, plane, origin):
+        return pltpu.make_async_remote_copy(
+            src_ref=src.at[plane], dst_ref=dst.at[origin],
+            send_sem=send_sem.at[which, plane], recv_sem=recv_sem.at[which, origin],
+            device_id=(tx, ty, plane), device_id_type=MESH,
+        )
+
+    def exchange(order):
+        for plane, band_of in order:
+            @pl.when(plane != me)
+            def _(plane=plane, band_of=band_of):
+                piece(*band_of, plane, me).start()
+
+    def gathered(which, src, dst):
+        total = src[me]
+        for d in range(1, n_ang):
+            origin = lax.rem(me + d, n_ang)
+            piece(which, src, dst, me, origin).wait_recv()
+            total += dst[origin]
         return total
 
-    bottom = gathered(0, bot, bot_in)
-    bot_sum[...] = bottom
+    def straight(plane, origin):
+        return pltpu.make_async_remote_copy(
+            src_ref=bot.at[plane], dst_ref=cross_in.at[origin],
+            send_sem=send_sem.at[2, plane], recv_sem=recv_sem.at[2, origin],
+            device_id=(tx, ty + 1, plane), device_id_type=MESH,
+        )
+
     down = pltpu.make_async_remote_copy(
-        src_ref=bot_sum, dst_ref=below_in, send_sem=send_sem.at[0], recv_sem=recv_sem.at[0],
-        device_id=(tx, ty_next, me), device_id_type=MESH,
+        src_ref=bot_sum, dst_ref=below_buf, send_sem=send_sem.at[3, 0], recv_sem=recv_sem.at[3, 0],
+        device_id=(tx, ty + 1, me), device_id_type=MESH,
     )
     across = pltpu.make_async_remote_copy(
-        src_ref=bot_sum.at[:, pl.ds(0, BLOCK)], dst_ref=corner_in,
-        send_sem=send_sem.at[n_ang], recv_sem=recv_sem.at[n_ang],
-        device_id=(tx_prev, ty_next, me), device_id_type=MESH,
+        src_ref=below_buf.at[:, pl.ds(0, BLOCK)], dst_ref=corner_in,
+        send_sem=send_sem.at[3, 1], recv_sem=recv_sem.at[3, 1],
+        device_id=(tx_prev, ty, me), device_id_type=MESH,
     )
-    across.start()
-    down.start()
+
+    @pl.when(late)
+    def _():
+        pl.semaphore_signal(ready_sem, inc=1, device_id=(tx, ty - 1, me), device_id_type=MESH)
+
+    @pl.when(late_sends)
+    def _():
+        for plane in range(n_ang):
+            straight(plane, me).start()
+
+    @pl.when(early)
+    def _():
+        exchange([(p, b) for p in range(3) for b in bands] + [(p, b) for b in bands for p in range(3, n_ang)])
+
+    @pl.when(late)
+    def _():
+        exchange([(p, b) for b in bands for p in range(n_ang)])
+
+    bottom = gathered(*bands[0])
+    bot_sum[...] = bottom
+    @pl.when(early)
+    def _():
+        pl.semaphore_wait(ready_sem, 1)
+        down.start()
 
     lower_ref[:, :F] = bottom[:band]
     lower_ref[:, F:] = pltpu.roll(bottom, band, 0)[:band]
-    own_top = gathered(1, top, top_in)
-
+    top_sum[...] = gathered(*bands[1])
+
+    @pl.when(late)
+    def _():
+        down.wait_recv()
+
+    @pl.when(early & has_above)
+    def _():
+        total = None
+        for origin in range(n_ang):
+            straight(me, origin).wait_recv()
+            total = cross_in[origin] if total is None else total + cross_in[origin]
+        below_buf[...] = total
+
+    @pl.when(ty == 0)
+    def _():
+        below_buf[...] = jnp.zeros_like(below_buf)
+
+    @pl.when(has_above)
+    def _():
+        across.start()
+
+    for copy in small[2:]:
+        copy.wait()
     row = sub % band
     own = jnp.zeros((8, BLOCK), jnp.float32)
     other = jnp.zeros((8, BLOCK), jnp.float32)
@@ -242,10 +320,13 @@
     shift = offset_ref[0, 0]
     turn_by = (BLOCK - shift) & (BLOCK - 1)
 
-    across.wait_recv()
-    down.wait_recv()
-    below = below_in[...]
-    corner = jnp.where(tx < n_tx - 1, corner_in[...], 0.0)
+    @pl.when(has_above)
+    def _():
+        across.wait_recv()
+
+    own_top = top_sum[...]
+    below = below_buf[...]
+    corner = jnp.where((tx < n_tx - 1) & has_above, corner_in[...], 0.0)
     tail = pltpu.roll(jnp.where(sub < band, corner, below[:, :BLOCK]), band, 0)
     pieces = [below[:, BLOCK * i : BLOCK * (i + 1)] for i in range(4)] + [tail]
     turned = [pltpu.roll(piece, turn_by, 1) for piece in pieces]
@@ -255,11 +336,33 @@
         seams_ref[:, BLOCK * i : BLOCK * (i + 1)] = seam[:band]
         seams_ref[:, F + BLOCK * i : F + BLOCK * (i + 1)] = pltpu.roll(seam, band, 0)[:band]
 
-    for group in copies:
-        for copy in group:
-            copy.wait_send()
-    across.wait_send()
-    down.wait_send()
+    for band_of in bands:
+        for d in range(1, n_ang):
+            piece(*band_of, lax.rem(me + d, n_ang), me).wait_send()
+
+    @pl.when(late_sends)
+    def _():
+        for plane in range(n_ang):
+            straight(plane, me).wait_send()
+
+    @pl.when(early)
+    def _():
+        down.wait_send()
+
+    @pl.when(has_above)
+    def _():
+        across.wait_send()
+
+
+def hand_over(seams_in, lower_in, seams_ref, lower_ref, sem):
+    copies = [
+        pltpu.make_async_copy(seams_in, seams_ref, sem.at[0]),
+        pltpu.make_async_copy(lower_in, lower_ref, sem.at[1]),
+    ]
+    for copy in copies:
+        copy.start()
+    for copy in copies:
+        copy.wait()
 
 
 def solution(mesh):
@@ -271,16 +374,20 @@
         band = rows // 2
         g = jnp.asarray(forward_half_table())
         t = jnp.asarray(inverse_half_tables(views * n_ang))
-        smem = pl.BlockSpec(memory_space=pltpu.SMEM)
         vmem = pl.BlockSpec(memory_space=pltpu.VMEM)
-        hbm = pl.BlockSpec(memory_space=pl.ANY)
+        hbm = pl.BlockSpec(memory_space=pltpu.HBM)
         f32 = jnp.float32
-        seams, lower = pl.pallas_call(
+        results = pl.pallas_call(
             functools.partial(kernel, sizes, views),
-            out_shape=[jax.ShapeDtypeStruct((band, width), f32)] * 2,
-            in_specs=[hbm, hbm, hbm, vmem, smem, smem, smem, smem],
+            out_shape=[pltpu.VMEM((band, width), f32)] * 2,
+            in_specs=[hbm] * 8,
             out_specs=[vmem, vmem],
             scratch_shapes=[
+                pltpu.VMEM((1, views), f32),
+                pltpu.SMEM((1, 1), f32),
+                pltpu.SMEM((1, 1), jnp.int32),
+                pltpu.SMEM((1, 1), jnp.int32),
+                pltpu.SMEM((1, 2, band), jnp.int32),
                 pltpu.VMEM((views, rows, width), jnp.bfloat16),
                 pltpu.VMEM((F, width), jnp.bfloat16),
                 pltpu.VMEM((2, F, F), jnp.bfloat16),
@@ -293,17 +400,29 @@
                 pltpu.VMEM((2, n_ang * rows, F), f32),
                 pltpu.VMEM((n_ang, rows, F), f32),
                 pltpu.VMEM((n_ang, rows, F), f32),
-                pltpu.VMEM((n_ang - 1, rows, F), f32),
-                pltpu.VMEM((n_ang - 1, rows, F), f32),
+                pltpu.VMEM((n_ang, rows, F), f32),
+                pltpu.VMEM((n_ang, rows, F), f32),
                 pltpu.VMEM((rows, F), f32),
+                pltpu.VMEM((rows, F), f32),
+                pltpu.VMEM((n_ang, rows, F), f32),
                 pltpu.VMEM((rows, F), f32),
                 pltpu.VMEM((rows, BLOCK), f32),
                 pltpu.SemaphoreType.DMA((3,)),
-                pltpu.SemaphoreType.DMA((2 * n_ang,)),
-                pltpu.SemaphoreType.DMA((2 * n_ang,)),
+                pltpu.SemaphoreType.DMA((5,)),
+                pltpu.SemaphoreType.DMA((4, n_ang)),
+                pltpu.SemaphoreType.DMA((4, n_ang)),
+                pltpu.SemaphoreType.REGULAR,
             ],
             compiler_params=pltpu.CompilerParams(collective_id=0, has_side_effects=True),
         )(projections[0, 0], g, t, view_angles[0], tilt, offsets, extents, feather[0])
+        anywhere = pl.BlockSpec(memory_space=pl.ANY)
+        seams, lower = pl.pallas_call(
+            hand_over,
+            out_shape=[jax.ShapeDtypeStruct((band, width), f32)] * 2,
+            in_specs=[anywhere] * 2,
+            out_specs=[anywhere] * 2,
+            scratch_shapes=[pltpu.SemaphoreType.DMA((2,))],
+        )(*(pltpu.with_memory_space_constraint(r, pltpu.VMEM) for r in results))
         return (seams[None, None, None], lower[None, None, None])
 
     in_specs = (

time: 41.6 us -> 32.5 us (0.78)
  the two profiles are of different devices: /device:TPU:1 before, /device:TPU:355 now
where the time goes in v2:
time: 32.5 us; the launch traced here: 32.3 us
  Pallas kernels  29.7 us (91%)
  between operations  2.57 us (8%)
    pallas_call x1, Pallas kernels, on_device(): pl.pallas_call(functools.partial(kernel, sizes, views), out_shape=[pltpu....  29.1 us

profile of v2, /device:TPU:355, one launch (start us, length us, event | category | flops | bytes accessed | tf_op | source)
XLA Modules:
  0.0 32.3 jit_solution(13565199172574688649)
XLA Ops:
  2.6 29.1 %shard_map.95 = (f32[4,1024]{1,0:T(4,128)S(1)}, f32[4,1024]{1,0:T(4,128)S(1)}) custom-call(bf16[16,8,1024]{2,1,0:T(8,128)(2,1)} %bitcast.5, bf16[512,1024]{1,0:T(8,128)(2,1)} %constant.4.clone.g_hbm, bf16[2,512,512]{2,1,0:T(8,128)(2,1)} %constant.5.clone.t_hbm, f32[1,16]{1,0:T(1,128)} %bitcast.7, f32[1,1]{1,0:T(1,128)S(6)} %copy.10.tilt_hbm, ...), custom_call_target="tpu_custom_call" | custom-call | tf_op jit(solution)/shard_map/pallas_call | solution.py:380
  31.7 0.6 %shard_map.96 = (f32[4,1024]{1,0:T(4,128)}, f32[4,1024]{1,0:T(4,128)}) custom-call(f32[4,1024]{1,0:T(4,128)S(1)} %get-tuple-element.6.seams_in, f32[4,1024]{1,0:T(4,128)S(1)} %get-tuple-element.7.lower_in), custom_call_target="tpu_custom_call" | custom-call | tf_op jit(solution)/shard_map/pallas_call | solution.py:419

commit v3 on v2

--- a/solution.py
+++ b/solution.py
@@ -73,7 +73,8 @@
     x_hbm, g_hbm, t_hbm, angles_hbm, tilt_hbm, offset_hbm, extent_hbm, feather_hbm,
     seams_ref, lower_ref,
     angles_ref, tilt_ref, offset_ref, extent_ref, feather_ref, x_buf, g_buf, t_buf, spec_buf, ycos, ysin, zcos, zsin, col_buf, q_buf,
-    bot, top, bot_in, top_in, bot_sum, top_sum, cross_in, below_buf, corner_in,
+    bot, top, bot_near, top_near, bot_pair, top_pair, bot_mid, top_mid, bot_four, top_four, bot_last, top_last, bot_far, top_far,
+    bot_sum, top_sum, cross_in, corners_in, below_buf, corner_sum,
     load_sem, small_sem, send_sem, recv_sem, ready_sem,
 ):
     n_tx, n_ty, n_ang = sizes
@@ -88,21 +89,28 @@
     def greet(*device):
         pl.semaphore_signal(barrier, inc=1, device_id=device, device_id_type=MESH)
 
-    for d in range(1, n_ang):
-        greet(tx, ty, lax.rem(me + d, n_ang))
-
-    @pl.when(has_above)
+    bits = [lax.rem(me, 2), lax.rem(me // 2, 2), me // 4]
+    partners = [me + step * (1 - 2 * bit) for step, bit in zip((1, 2, 4), bits)]
+    half, parity = me // 2, bits[0]
+    n_pair = n_ang // 2
+    greet(tx, ty, partners[0])
+    greet(tx, ty, partners[1])
+    greet(tx, ty, partners[2])
+
+    @pl.when(late)
     def _():
         greet(tx_next, ty, me)
 
     @pl.when(early)
     def _():
+        greet(tx, ty, partners[1] + partners[2] - me)
         greet(tx, ty + 1, me)
 
     @pl.when(early & has_above)
     def _():
-        for a in range(n_ang):
-            greet(tx, ty - 1, a)
+        for i in range(n_pair):
+            greet(tx, ty - 1, 2 * i + parity)
+            greet(tx_next, ty - 1, 2 * i + parity)
 
     small = [
         pltpu.make_async_copy(src, dst, small_sem.at[n])
@@ -213,46 +221,96 @@
         bot[plane] = jnp.where(upper, pltpu.roll(a, band, 0), b)
         top[plane] = jnp.where(upper, a, pltpu.roll(b, band, 0))
 
-    greeted = n_ang - 1 + has_above.astype(jnp.int32) + late.astype(jnp.int32)
-    pl.semaphore_wait(barrier, greeted + n_ang * late_sends.astype(jnp.int32))
-
-    bands = ((0, bot, bot_in), (1, top, top_in))
-
-    def piece(which, src, dst, plane, origin):
+    greeted = n_pair + late.astype(jnp.int32)
+    pl.semaphore_wait(barrier, greeted + 2 * n_pair * late_sends.astype(jnp.int32))
+
+    bands = (
+        (0, bot, bot_near, bot_pair, bot_mid, bot_four, bot_last),
+        (1, top, top_near, top_pair, top_mid, top_four, top_last),
+    )
+    far_slots = (bot_far, top_far)
+
+    def swap(src, dst, sem, partner):
         return pltpu.make_async_remote_copy(
-            src_ref=src.at[plane], dst_ref=dst.at[origin],
-            send_sem=send_sem.at[which, plane], recv_sem=recv_sem.at[which, origin],
-            device_id=(tx, ty, plane), device_id_type=MESH,
+            src_ref=src, dst_ref=dst, send_sem=send_sem.at[sem], recv_sem=recv_sem.at[sem],
+            device_id=(tx, ty, partner), device_id_type=MESH,
         )
 
-    def exchange(order):
-        for plane, band_of in order:
-            @pl.when(plane != me)
-            def _(plane=plane, band_of=band_of):
-                piece(*band_of, plane, me).start()
-
-    def gathered(which, src, dst):
-        total = src[me]
-        for d in range(1, n_ang):
-            origin = lax.rem(me + d, n_ang)
-            piece(which, src, dst, me, origin).wait_recv()
-            total += dst[origin]
+    def near(band_of, i):
+        which, mine, landed = band_of[:3]
+        return swap(mine.at[2 * i + 1 - parity], landed.at[i], 7 * which + i, partners[0])
+
+    def mid(band_of, j):
+        which, pair, landed = band_of[0], band_of[3], band_of[4]
+        return swap(pair.at[2 * j + 1 - bits[1]], landed.at[j], 7 * which + 4 + j, partners[1])
+
+    def last(band_of):
+        which, four, landed = band_of[0], band_of[5], band_of[6]
+        return swap(four.at[1 - bits[2]], landed, 7 * which + 6, partners[2])
+
+    def paired(band_of, i):
+        _, mine, landed, pair = band_of[:4]
+        near(band_of, i).wait_recv()
+        pair[i] = mine[2 * i + parity] + landed[i]
+
+    def send_mid(band_of):
+        for j in range(n_pair // 2):
+            mid(band_of, j).start()
+
+    def send_last(band_of):
+        _, _, _, pair, landed, four, _ = band_of
+        for j in range(n_pair // 2):
+            mid(band_of, j).wait_recv()
+            four[j] = pair[2 * j + bits[1]] + landed[j]
+        last(band_of).start()
+
+    def gathered(band_of):
+        four, landed = band_of[5:]
+        last(band_of).wait_recv()
+        return four[bits[2]] + landed[...]
+
+    def far(band_of, i, origin):
+        which, pair = band_of[0], band_of[3]
+        return pltpu.make_async_remote_copy(
+            src_ref=pair.at[i], dst_ref=far_slots[which].at[origin],
+            send_sem=send_sem.at[24 + 4 * which + i], recv_sem=recv_sem.at[24 + 4 * which + origin],
+            device_id=(tx, ty, 2 * i + parity), device_id_type=MESH,
+        )
+
+    def send_far(band_of, i):
+        @pl.when(i != half)
+        def _():
+            far(band_of, i, half).start()
+
+    def gathered_far(band_of):
+        total = band_of[3][half]
+        for d in range(1, n_pair):
+            origin = lax.rem(half + d, n_pair)
+            far(band_of, half, origin).wait_recv()
+            total += far_slots[band_of[0]][origin]
         return total
 
-    def straight(plane, origin):
+    def straight(i, origin):
         return pltpu.make_async_remote_copy(
-            src_ref=bot.at[plane], dst_ref=cross_in.at[origin],
-            send_sem=send_sem.at[2, plane], recv_sem=recv_sem.at[2, origin],
-            device_id=(tx, ty + 1, plane), device_id_type=MESH,
+            src_ref=bot_pair.at[i], dst_ref=cross_in.at[origin],
+            send_sem=send_sem.at[14 + i], recv_sem=recv_sem.at[14 + origin],
+            device_id=(tx, ty + 1, 2 * i + parity), device_id_type=MESH,
         )
 
+    def slanted(i, origin):
+        return pltpu.make_async_remote_copy(
+            src_ref=bot_pair.at[i, :, pl.ds(0, BLOCK)], dst_ref=corners_in.at[origin],
+            send_sem=send_sem.at[18 + i], recv_sem=recv_sem.at[18 + origin],
+            device_id=(tx_prev, ty + 1, 2 * i + parity), device_id_type=MESH,
+        )
+
     down = pltpu.make_async_remote_copy(
-        src_ref=bot_sum, dst_ref=below_buf, send_sem=send_sem.at[3, 0], recv_sem=recv_sem.at[3, 0],
+        src_ref=bot_sum, dst_ref=below_buf, send_sem=send_sem.at[22], recv_sem=recv_sem.at[22],
         device_id=(tx, ty + 1, me), device_id_type=MESH,
     )
     across = pltpu.make_async_remote_copy(
-        src_ref=below_buf.at[:, pl.ds(0, BLOCK)], dst_ref=corner_in,
-        send_sem=send_sem.at[3, 1], recv_sem=recv_sem.at[3, 1],
+        src_ref=below_buf.at[:, pl.ds(0, BLOCK)], dst_ref=corners_in.at[0],
+        send_sem=send_sem.at[23], recv_sem=recv_sem.at[23],
         device_id=(tx_prev, ty, me), device_id_type=MESH,
     )
 
@@ -260,29 +318,44 @@
     def _():
         pl.semaphore_signal(ready_sem, inc=1, device_id=(tx, ty - 1, me), device_id_type=MESH)
 
-    @pl.when(late_sends)
-    def _():
-        for plane in range(n_ang):
-            straight(plane, me).start()
+    lower_part, upper_part = bands
+    for band_of in bands:
+        for i in range(n_pair):
+            near(band_of, i).start()
+
+    @pl.when(late)
+    def _():
+        for i in range(n_pair):
+            paired(lower_part, i)
+
+            @pl.when(late_sends)
+            def _():
+                slanted(i, half).start()
+                straight(i, half).start()
+
+        send_mid(lower_part)
+        for i in range(n_pair):
+            paired(upper_part, i)
+        send_mid(upper_part)
+        send_last(lower_part)
+        send_last(upper_part)
+        bot_sum[...] = gathered(lower_part)
+        top_sum[...] = gathered(upper_part)
 
     @pl.when(early)
     def _():
-        exchange([(p, b) for p in range(3) for b in bands] + [(p, b) for b in bands for p in range(3, n_ang)])
-
-    @pl.when(late)
-    def _():
-        exchange([(p, b) for b in bands for p in range(n_ang)])
-
-    bottom = gathered(*bands[0])
-    bot_sum[...] = bottom
-    @pl.when(early)
-    def _():
+        for band_of in bands:
+            for i in range(n_pair):
+                paired(band_of, i)
+                send_far(band_of, i)
+        bot_sum[...] = gathered_far(lower_part)
         pl.semaphore_wait(ready_sem, 1)
         down.start()
-
+        top_sum[...] = gathered_far(upper_part)
+
+    bottom = bot_sum[...]
     lower_ref[:, :F] = bottom[:band]
     lower_ref[:, F:] = pltpu.roll(bottom, band, 0)[:band]
-    top_sum[...] = gathered(*bands[1])
 
     @pl.when(late)
     def _():
@@ -290,17 +363,18 @@
 
     @pl.when(early & has_above)
     def _():
-        total = None
-        for origin in range(n_ang):
-            straight(me, origin).wait_recv()
-            total = cross_in[origin] if total is None else total + cross_in[origin]
-        below_buf[...] = total
+        for origin in range(n_pair):
+            slanted(half, origin).wait_recv()
+            straight(half, origin).wait_recv()
+        below_buf[...] = (cross_in[0] + cross_in[1]) + (cross_in[2] + cross_in[3])
+        corner_sum[...] = (corners_in[0] + corners_in[1]) + (corners_in[2] + corners_in[3])
 
     @pl.when(ty == 0)
     def _():
         below_buf[...] = jnp.zeros_like(below_buf)
-
-    @pl.when(has_above)
+        corner_sum[...] = jnp.zeros_like(corner_sum)
+
+    @pl.when(late)
     def _():
         across.start()
 
@@ -320,13 +394,14 @@
     shift = offset_ref[0, 0]
     turn_by = (BLOCK - shift) & (BLOCK - 1)
 
-    @pl.when(has_above)
+    @pl.when(late)
     def _():
         across.wait_recv()
+        corner_sum[...] = corners_in[0]
 
     own_top = top_sum[...]
     below = below_buf[...]
-    corner = jnp.where((tx < n_tx - 1) & has_above, corner_in[...], 0.0)
+    corner = jnp.where(tx < n_tx - 1, corner_sum[...], 0.0)
     tail = pltpu.roll(jnp.where(sub < band, corner, below[:, :BLOCK]), band, 0)
     pieces = [below[:, BLOCK * i : BLOCK * (i + 1)] for i in range(4)] + [tail]
     turned = [pltpu.roll(piece, turn_by, 1) for piece in pieces]
@@ -337,19 +412,31 @@
         seams_ref[:, F + BLOCK * i : F + BLOCK * (i + 1)] = pltpu.roll(seam, band, 0)[:band]
 
     for band_of in bands:
-        for d in range(1, n_ang):
-            piece(*band_of, lax.rem(me + d, n_ang), me).wait_send()
+        for i in range(n_pair):
+            near(band_of, i).wait_send()
+
+        @pl.when(late)
+        def _():
+            for j in range(n_pair // 2):
+                mid(band_of, j).wait_send()
+            last(band_of).wait_send()
+
+        @pl.when(early)
+        def _():
+            for d in range(1, n_pair):
+                far(band_of, lax.rem(half + d, n_pair), half).wait_send()
 
     @pl.when(late_sends)
     def _():
-        for plane in range(n_ang):
-            straight(plane, me).wait_send()
+        for i in range(n_pair):
+            slanted(i, half).wait_send()
+            straight(i, half).wait_send()
 
     @pl.when(early)
     def _():
         down.wait_send()
 
-    @pl.when(has_above)
+    @pl.when(late)
     def _():
         across.wait_send()
 
@@ -400,17 +487,19 @@
                 pltpu.VMEM((2, n_ang * rows, F), f32),
                 pltpu.VMEM((n_ang, rows, F), f32),
                 pltpu.VMEM((n_ang, rows, F), f32),
-                pltpu.VMEM((n_ang, rows, F), f32),
-                pltpu.VMEM((n_ang, rows, F), f32),
-                pltpu.VMEM((rows, F), f32),
-                pltpu.VMEM((rows, F), f32),
-                pltpu.VMEM((n_ang, rows, F), f32),
+                *[pltpu.VMEM((n_ang // 2, rows, F), f32)] * 4,
+                *[pltpu.VMEM((n_ang // 4, rows, F), f32)] * 4,
+                *[pltpu.VMEM((rows, F), f32)] * 2,
+                *[pltpu.VMEM((n_ang // 2, rows, F), f32)] * 2,
+                *[pltpu.VMEM((rows, F), f32)] * 2,
+                pltpu.VMEM((n_ang // 2, rows, F), f32),
+                pltpu.VMEM((n_ang // 2, rows, BLOCK), f32),
                 pltpu.VMEM((rows, F), f32),
                 pltpu.VMEM((rows, BLOCK), f32),
                 pltpu.SemaphoreType.DMA((3,)),
                 pltpu.SemaphoreType.DMA((5,)),
-                pltpu.SemaphoreType.DMA((4, n_ang)),
-                pltpu.SemaphoreType.DMA((4, n_ang)),
+                pltpu.SemaphoreType.DMA((32,)),
+                pltpu.SemaphoreType.DMA((32,)),
                 pltpu.SemaphoreType.REGULAR,
             ],
             compiler_params=pltpu.CompilerParams(collective_id=0, has_side_effects=True),

time: 32.5 us -> 30.4 us (0.935)
  the two profiles are of different devices: /device:TPU:355 before, /device:TPU:75 now
where the time goes in v3:
time: 30.4 us; the launch traced here: 30.2 us
  Pallas kernels  27.7 us (91%)
  between operations  2.57 us (8%)
    pallas_call x1, Pallas kernels, on_device(): pl.pallas_call(functools.partial(kernel, sizes, views), out_shape=[pltpu....  27 us
    pallas_call x1, Pallas kernels, on_device(): pl.pallas_call(hand_over, out_shape=[jax.ShapeDtypeStruct((band, width),...  0.63 us

profile of v3, /device:TPU:75, one launch (start us, length us, event | category | flops | bytes accessed | tf_op | source)
XLA Modules:
  0.0 30.2 jit_solution(8804717945759103012)
XLA Ops:
  2.6 27.0 %shard_map.95 = (f32[4,1024]{1,0:T(4,128)S(1)}, f32[4,1024]{1,0:T(4,128)S(1)}) custom-call(bf16[16,8,1024]{2,1,0:T(8,128)(2,1)} %bitcast.5, bf16[512,1024]{1,0:T(8,128)(2,1)} %constant.4.clone.g_hbm, bf16[2,512,512]{2,1,0:T(8,128)(2,1)} %constant.5.clone.t_hbm, f32[1,16]{1,0:T(1,128)} %bitcast.7, f32[1,1]{1,0:T(1,128)S(6)} %copy.10.tilt_hbm, ...), custom_call_target="tpu_custom_call" | custom-call | tf_op jit(solution)/shard_map/pallas_call | solution.py:467
  29.6 0.6 %shard_map.96 = (f32[4,1024]{1,0:T(4,128)}, f32[4,1024]{1,0:T(4,128)}) custom-call(f32[4,1024]{1,0:T(4,128)S(1)} %get-tuple-element.6.seams_in, f32[4,1024]{1,0:T(4,128)S(1)} %get-tuple-element.7.lower_in), custom_call_target="tpu_custom_call" | custom-call | tf_op jit(solution)/shard_map/pallas_call | solution.py:508

commit v4 on v3

--- a/solution.py
+++ b/solution.py
@@ -84,34 +84,6 @@
     has_above = ty > 0
     late_sends = late & (ty < n_ty - 1)
 
-    barrier = pltpu.get_barrier_semaphore()
-
-    def greet(*device):
-        pl.semaphore_signal(barrier, inc=1, device_id=device, device_id_type=MESH)
-
-    bits = [lax.rem(me, 2), lax.rem(me // 2, 2), me // 4]
-    partners = [me + step * (1 - 2 * bit) for step, bit in zip((1, 2, 4), bits)]
-    half, parity = me // 2, bits[0]
-    n_pair = n_ang // 2
-    greet(tx, ty, partners[0])
-    greet(tx, ty, partners[1])
-    greet(tx, ty, partners[2])
-
-    @pl.when(late)
-    def _():
-        greet(tx_next, ty, me)
-
-    @pl.when(early)
-    def _():
-        greet(tx, ty, partners[1] + partners[2] - me)
-        greet(tx, ty + 1, me)
-
-    @pl.when(early & has_above)
-    def _():
-        for i in range(n_pair):
-            greet(tx, ty - 1, 2 * i + parity)
-            greet(tx_next, ty - 1, 2 * i + parity)
-
     small = [
         pltpu.make_async_copy(src, dst, small_sem.at[n])
         for n, (src, dst) in enumerate((
@@ -127,6 +99,34 @@
     load_x.start()
     load_g.start()
     load_t.start()
+
+    barrier = pltpu.get_barrier_semaphore()
+
+    def greet(*device):
+        pl.semaphore_signal(barrier, inc=1, device_id=device, device_id_type=MESH)
+
+    bits = [lax.rem(me, 2), lax.rem(me // 2, 2), me // 4]
+    partners = [me + step * (1 - 2 * bit) for step, bit in zip((1, 2, 4), bits)]
+    half, parity = me // 2, bits[0]
+    n_pair = n_ang // 2
+    greet(tx, ty, partners[0])
+    greet(tx, ty, partners[1])
+    greet(tx, ty, partners[2])
+
+    @pl.when(late)
+    def _():
+        greet(tx_next, ty, me)
+
+    @pl.when(early)
+    def _():
+        greet(tx, ty, partners[1] + partners[2] - me)
+        greet(tx, ty + 1, me)
+
+    @pl.when(early & has_above)
+    def _():
+        for i in range(n_pair):
+            greet(tx, ty - 1, 2 * i + parity)
+            greet(tx_next, ty - 1, 2 * i + parity)
 
     small[0].wait()
     small[1].wait()
@@ -253,21 +253,20 @@
         near(band_of, i).wait_recv()
         pair[i] = mine[2 * i + parity] + landed[i]
 
-    def send_mid(band_of):
-        for j in range(n_pair // 2):
-            mid(band_of, j).start()
+    def four(band_of, j):
+        _, _, _, pair, landed, fours, _ = band_of
+        mid(band_of, j).wait_recv()
+        fours[j] = pair[2 * j + bits[1]] + landed[j]
 
     def send_last(band_of):
-        _, _, _, pair, landed, four, _ = band_of
-        for j in range(n_pair // 2):
-            mid(band_of, j).wait_recv()
-            four[j] = pair[2 * j + bits[1]] + landed[j]
+        four(band_of, 1 - bits[2])
         last(band_of).start()
 
     def gathered(band_of):
-        four, landed = band_of[5:]
+        fours, landed = band_of[5:]
+        four(band_of, bits[2])
         last(band_of).wait_recv()
-        return four[bits[2]] + landed[...]
+        return fours[bits[2]] + landed[...]
 
     def far(band_of, i, origin):
         which, pair = band_of[0], band_of[3]
@@ -299,7 +298,7 @@
 
     def slanted(i, origin):
         return pltpu.make_async_remote_copy(
-            src_ref=bot_pair.at[i, :, pl.ds(0, BLOCK)], dst_ref=corners_in.at[origin],
+            src_ref=bot_pair.at[i, pl.ds(0, 4), pl.ds(0, BLOCK)], dst_ref=corners_in.at[origin, pl.ds(0, 4)],
             send_sem=send_sem.at[18 + i], recv_sem=recv_sem.at[18 + origin],
             device_id=(tx_prev, ty + 1, 2 * i + parity), device_id_type=MESH,
         )
@@ -319,13 +318,25 @@
         pl.semaphore_signal(ready_sem, inc=1, device_id=(tx, ty - 1, me), device_id_type=MESH)
 
     lower_part, upper_part = bands
-    for band_of in bands:
-        for i in range(n_pair):
-            near(band_of, i).start()
-
-    @pl.when(late)
-    def _():
-        for i in range(n_pair):
+    held = [late & (parity == 0) & (half < 2), late & (parity == 0) & (half >= 2)]
+    plans = ({2: (0, 1, 2, 3)}, {1: (1, 2), 2: (3,)})
+    for i in range(n_pair):
+        near(lower_part, i).start()
+
+    for i in range(n_pair):
+        @pl.when((late & (parity == 1)) | (held[1] & (i < 1)))
+        def _():
+            near(upper_part, i).start()
+
+    @pl.when(late)
+    def _():
+        for i in range(n_pair):
+            for group, plan in zip(held, plans):
+                @pl.when(group)
+                def _(plan=plan):
+                    for k in plan.get(i, ()):
+                        near(upper_part, k).start()
+
             paired(lower_part, i)
 
             @pl.when(late_sends)
@@ -333,10 +344,12 @@
                 slanted(i, half).start()
                 straight(i, half).start()
 
-        send_mid(lower_part)
+        for j in range(n_pair // 2):
+            mid(lower_part, j).start()
         for i in range(n_pair):
             paired(upper_part, i)
-        send_mid(upper_part)
+            if i % 2:
+                mid(upper_part, i // 2).start()
         send_last(lower_part)
         send_last(upper_part)
         bot_sum[...] = gathered(lower_part)
@@ -344,10 +357,15 @@
 
     @pl.when(early)
     def _():
-        for band_of in bands:
-            for i in range(n_pair):
-                paired(band_of, i)
-                send_far(band_of, i)
+        for i in range(n_pair):
+            paired(lower_part, i)
+            send_far(lower_part, i)
+            if i == 3:
+                for n in range(n_pair):
+                    near(upper_part, n).start()
+        for i in range(n_pair):
+            paired(upper_part, i)
+            send_far(upper_part, i)
         bot_sum[...] = gathered_far(lower_part)
         pl.semaphore_wait(ready_sem, 1)
         down.start()

time: 30.4 us -> 29.6 us (0.974)
  the two profiles are of different devices: /device:TPU:75 before, /device:TPU:461 now
where the time goes in v4:
time: 29.6 us; the launch traced here: 29.4 us
  Pallas kernels  26.8 us (91%)
  between operations  2.57 us (9%)
    pallas_call x1, Pallas kernels, on_device(): pl.pallas_call(functools.partial(kernel, sizes, views), out_shape=[pltpu....  26.2 us
    pallas_call x1, Pallas kernels, on_device(): pl.pallas_call(hand_over, out_shape=[jax.ShapeDtypeStruct((band, width),...  0.63 us

profile of v4, /device:TPU:461, one launch (start us, length us, event | category | flops | bytes accessed | tf_op | source)
XLA Modules:
  0.0 29.4 jit_solution(15668169670556830950)
XLA Ops:
  2.6 26.2 %shard_map.95 = (f32[4,1024]{1,0:T(4,128)S(1)}, f32[4,1024]{1,0:T(4,128)S(1)}) custom-call(bf16[16,8,1024]{2,1,0:T(8,128)(2,1)} %bitcast.5, bf16[512,1024]{1,0:T(8,128)(2,1)} %constant.4.clone.g_hbm, bf16[2,512,512]{2,1,0:T(8,128)(2,1)} %constant.5.clone.t_hbm, f32[1,16]{1,0:T(1,128)} %bitcast.7, f32[1,1]{1,0:T(1,128)S(6)} %copy.10.tilt_hbm, ...), custom_call_target="tpu_custom_call" | custom-call | tf_op jit(solution)/shard_map/pallas_call | solution.py:485
  28.8 0.6 %shard_map.96 = (f32[4,1024]{1,0:T(4,128)}, f32[4,1024]{1,0:T(4,128)}) custom-call(f32[4,1024]{1,0:T(4,128)S(1)} %get-tuple-element.6.seams_in, f32[4,1024]{1,0:T(4,128)S(1)} %get-tuple-element.7.lower_in), custom_call_target="tpu_custom_call" | custom-call | tf_op jit(solution)/shard_map/pallas_call | solution.py:526

commit v5 on v4

--- a/solution.py
+++ b/solution.py
@@ -21,17 +21,15 @@
 COS_HALF = (0.9999999532476085, -4.934792830619664, 4.058411352862771, -1.3318765680813944, 0.21968961109803095)
 
 
-def frequency_order():
-    return np.concatenate([np.arange(0, F, 2), np.arange(1, F, 2)])
-
-
-def forward_half_table():
-    freq = frequency_order()[None, :]
+def forward_half_tables():
     column = np.arange(U // 2)[:, None]
-    turn = (column * freq % U) * (2.0 * math.pi / U)
-    filt = (freq + 0.5) / F / math.sqrt(U)
-    both = np.concatenate([np.cos(turn) * filt, -np.sin(turn) * filt], axis=1)
-    return both.astype(np.float32).astype(ml_dtypes.bfloat16)
+    halves = []
+    for start in (0, 1):
+        freq = np.arange(start, F, 2)[None, :]
+        turn = (column * freq % U) * (2.0 * math.pi / U)
+        filt = (freq + 0.5) / F / math.sqrt(U)
+        halves.append(np.concatenate([np.cos(turn) * filt, -np.sin(turn) * filt], axis=1))
+    return np.stack(halves).astype(np.float32).astype(ml_dtypes.bfloat16)
 
 
 def inverse_half_tables(views):
@@ -94,11 +92,11 @@
     for copy in small:
         copy.start()
     load_x = pltpu.make_async_copy(x_hbm, x_buf, load_sem.at[0])
-    load_g = pltpu.make_async_copy(g_hbm, g_buf, load_sem.at[1])
-    load_t = pltpu.make_async_copy(t_hbm, t_buf, load_sem.at[2])
+    load_g = [pltpu.make_async_copy(g_hbm.at[part], g_buf.at[part], load_sem.at[1 + part]) for part in range(2)]
+    load_t = [pltpu.make_async_copy(t_hbm.at[part], t_buf.at[part], load_sem.at[3 + part]) for part in range(2)]
     load_x.start()
-    load_g.start()
-    load_t.start()
+    for load in load_g + load_t:
+        load.start()
 
     barrier = pltpu.get_barrier_semaphore()
 
@@ -162,26 +160,28 @@
             ysin[8 * k : 8 * k + 8, at] = s
 
     load_x.wait()
-    load_g.wait()
     rows = views * 8
     left = x_buf[:, :, : U // 2].reshape(rows, U // 2)
     right = x_buf[:, :, U // 2 :].reshape(rows, U // 2)
-    spec_buf[...] = jnp.dot(
-        jnp.concatenate([left, right], axis=0), g_buf[...], preferred_element_type=jnp.float32
-    )
+    halves_of_x = jnp.concatenate([left, right], axis=0)
+    for part in range(2):
+        load_g[part].wait()
+        spec_buf[part] = jnp.dot(halves_of_x, g_buf[part], preferred_element_type=jnp.float32)
 
     for i in range(4):
         at = slice(BLOCK * i, BLOCK * (i + 1))
-        at_im = slice(F + BLOCK * i, F + BLOCK * (i + 1))
+        part, col = i // 2, BLOCK * (i % 2)
+        spec = spec_buf.at[part]
+        at_re, at_im = slice(col, col + BLOCK), slice(F // 2 + col, F // 2 + col + BLOCK)
         acc = [[jnp.zeros((8, BLOCK), jnp.float32) for _ in range(4)] for _ in range(4)]
         for k in range(views):
             here, there = slice(8 * k, 8 * k + 8), slice(rows + 8 * k, rows + 8 * k + 8)
             if i < 2:
-                s_re = spec_buf[here, at] + spec_buf[there, at]
-                s_im = spec_buf[here, at_im] + spec_buf[there, at_im]
+                s_re = spec[here, at_re] + spec[there, at_re]
+                s_im = spec[here, at_im] + spec[there, at_im]
             else:
-                s_re = spec_buf[here, at] - spec_buf[there, at]
-                s_im = spec_buf[here, at_im] - spec_buf[there, at_im]
+                s_re = spec[here, at_re] - spec[there, at_re]
+                s_im = spec[here, at_im] - spec[there, at_im]
             yc, ys = ycos[here, at], ysin[here, at]
             p_re = s_re * yc - s_im * ys
             p_im = s_re * ys + s_im * yc
@@ -192,7 +192,6 @@
                 acc[j][1] += c * p_im
                 acc[j][2] += s * p_re
                 acc[j][3] += s * p_im
-        part, col = i // 2, BLOCK * (i % 2)
         for j in range(4):
             c_re, c_im, s_re, s_im = acc[j]
             for plane, re, im in (
@@ -203,9 +202,9 @@
                 q_buf[part, at_row, col : col + BLOCK] = re
                 q_buf[part, at_row, F // 2 + col : F // 2 + col + BLOCK] = im
 
-    load_t.wait()
     halves = []
     for part in range(2):
+        load_t[part].wait()
         q = q_buf[part]
         high = q.astype(jnp.bfloat16)
         low = (q - high.astype(jnp.float32)).astype(jnp.bfloat16)
@@ -219,7 +218,6 @@
     for plane in range(8):
         a, b = first[8 * plane : 8 * plane + 8], second[8 * plane : 8 * plane + 8]
         bot[plane] = jnp.where(upper, pltpu.roll(a, band, 0), b)
-        top[plane] = jnp.where(upper, a, pltpu.roll(b, band, 0))
 
     greeted = n_pair + late.astype(jnp.int32)
     pl.semaphore_wait(barrier, greeted + 2 * n_pair * late_sends.astype(jnp.int32))
@@ -321,7 +319,11 @@
     held = [late & (parity == 0) & (half < 2), late & (parity == 0) & (half >= 2)]
     plans = ({2: (0, 1, 2, 3)}, {1: (1, 2), 2: (3,)})
     for i in range(n_pair):
-        near(lower_part, i).start()
+        near(lower_part, jnp.where(early, n_pair - 1 - i, i)).start()
+
+    for plane in range(8):
+        a, b = first[8 * plane : 8 * plane + 8], second[8 * plane : 8 * plane + 8]
+        top[plane] = jnp.where(upper, a, pltpu.roll(b, band, 0))
 
     for i in range(n_pair):
         @pl.when((late & (parity == 1)) | (held[1] & (i < 1)))
@@ -348,8 +350,11 @@
             mid(lower_part, j).start()
         for i in range(n_pair):
             paired(upper_part, i)
-            if i % 2:
+
+            @pl.when(bits[1] == 1 - i % 2)
+            def _():
                 mid(upper_part, i // 2).start()
+
         send_last(lower_part)
         send_last(upper_part)
         bot_sum[...] = gathered(lower_part)
@@ -357,12 +362,11 @@
 
     @pl.when(early)
     def _():
-        for i in range(n_pair):
+        for i in reversed(range(n_pair)):
             paired(lower_part, i)
             send_far(lower_part, i)
-            if i == 3:
-                for n in range(n_pair):
-                    near(upper_part, n).start()
+        for i in range(n_pair):
+            near(upper_part, i).start()
         for i in range(n_pair):
             paired(upper_part, i)
             send_far(upper_part, i)
@@ -477,7 +481,7 @@
     def on_device(projections, view_angles, tilt, offsets, extents, feather):
         _, _, views, rows, width = projections.shape
         band = rows // 2
-        g = jnp.asarray(forward_half_table())
+        g = jnp.asarray(forward_half_tables())
         t = jnp.asarray(inverse_half_tables(views * n_ang))
         vmem = pl.BlockSpec(memory_space=pltpu.VMEM)
         hbm = pl.BlockSpec(memory_space=pltpu.HBM)
@@ -494,9 +498,9 @@
                 pltpu.SMEM((1, 1), jnp.int32),
                 pltpu.SMEM((1, 2, band), jnp.int32),
                 pltpu.VMEM((views, rows, width), jnp.bfloat16),
-                pltpu.VMEM((F, width), jnp.bfloat16),
                 pltpu.VMEM((2, F, F), jnp.bfloat16),
-                pltpu.VMEM((2 * views * rows, width), f32),
+                pltpu.VMEM((2, F, F), jnp.bfloat16),
+                pltpu.VMEM((2, 2 * views * rows, F), f32),
                 pltpu.VMEM((views * rows, F), f32),
                 pltpu.VMEM((views * rows, F), f32),
                 pltpu.VMEM((4, views, F), f32),
@@ -514,7 +518,7 @@
                 pltpu.VMEM((n_ang // 2, rows, BLOCK), f32),
                 pltpu.VMEM((rows, F), f32),
                 pltpu.VMEM((rows, BLOCK), f32),
-                pltpu.SemaphoreType.DMA((3,)),
+                pltpu.SemaphoreType.DMA((5,)),
                 pltpu.SemaphoreType.DMA((5,)),
                 pltpu.SemaphoreType.DMA((32,)),
                 pltpu.SemaphoreType.DMA((32,)),

time: 29.6 us -> 29.1 us (0.983)
  the two profiles are of different devices: /device:TPU:461 before, /device:TPU:6 now
where the time goes in v5:
time: 29.1 us; the launch traced here: 28.9 us
  Pallas kernels  26.3 us (90%)
  between operations  2.57 us (9%)
    pallas_call x1, Pallas kernels, on_device(): pl.pallas_call(functools.partial(kernel, sizes, views), out_shape=[pltpu....  25.7 us
    pallas_call x1, Pallas kernels, on_device(): pl.pallas_call(hand_over, out_shape=[jax.ShapeDtypeStruct((band, width),...  0.63 us

profile of v5, /device:TPU:6, one launch (start us, length us, event | category | flops | bytes accessed | tf_op | source)
XLA Modules:
  0.0 28.9 jit_solution(938920558512767683)
XLA Ops:
  2.6 25.7 %shard_map.95 = (f32[4,1024]{1,0:T(4,128)S(1)}, f32[4,1024]{1,0:T(4,128)S(1)}) custom-call(bf16[16,8,1024]{2,1,0:T(8,128)(2,1)} %bitcast.5, bf16[2,512,512]{2,1,0:T(8,128)(2,1)} %constant.4.clone.g_hbm, bf16[2,512,512]{2,1,0:T(8,128)(2,1)} %constant.5.clone.t_hbm, f32[1,16]{1,0:T(1,128)} %bitcast.7, f32[1,1]{1,0:T(1,128)S(6)} %copy.10.tilt_hbm, ...), custom_call_target="tpu_custom_call" | custom-call | tf_op jit(solution)/shard_map/pallas_call | solution.py:489
  28.3 0.6 %shard_map.96 = (f32[4,1024]{1,0:T(4,128)}, f32[4,1024]{1,0:T(4,128)}) custom-call(f32[4,1024]{1,0:T(4,128)S(1)} %get-tuple-element.6.seams_in, f32[4,1024]{1,0:T(4,128)S(1)} %get-tuple-element.7.lower_in), custom_call_target="tpu_custom_call" | custom-call | tf_op jit(solution)/shard_map/pallas_call | solution.py:530
